TPU v7x, 32 devices: a whole 2x2x4 slice. The times are simulated.
32 devices in a mesh: section: 2 (over core), rep: 2 (over x), tp: 8 (over z, y).
Axes of the slice: x: 2, y: 2, z: 4, core: 2. Of those that a mesh axis runs over, the one named last changes fastest.
Arguments:
- states: bfloat16 [2, 2, 256, 8192], P('section', 'rep', None, 'tp'), may hold values from -6 to 6
- q_weight: bfloat16 [8192, 4096], P(None, 'tp'), may hold values from -0.0625 to 0.0625
- kv_weight: bfloat16 [8192, 1024], P('tp'), may hold values from -0.0625 to 0.0625
- o_weight: bfloat16 [4096, 8192], P(None, 'tp'), may hold values from -0.09375 to 0.09375
- store_keys: bfloat16 [2, 2, 4096, 512], P('section', 'rep', 'tp'), may hold values from -170 to 170
- store_values: bfloat16 [2, 2, 4096, 512], P('section', 'rep', 'tp'), may hold values from -48 to 48
- prefix_len: int32 [2], replicated, may hold values from 1024 to 4096
- cache_len: int32 [2, 4], P('rep'), may hold values from 128 to 1024
- parents: int32 [2, 4, 64], P('rep'), may hold values from -1 to 62, as said below
Outputs:
- attn_out: bfloat16 [2, 2, 256, 8192], P('section', 'rep', None, 'tp')
Inputs may be any that keep to these rules, and one draw needn't show every extreme that they name: `parents`: each node's parent is an earlier node of the same tree; only node 0 has -1.
All inputs are finite; a program needn't handle non-finite values.
Results may differ from a plain program's by a relative error of at most 0.0065.
The roundings to bfloat16 on the way count: a program that leaves them out, or rounds other values in their place, can miss the bound.
Values may be sent and summed in bfloat16 or wider, within the bound.
No kernel may reach another device: no remote copies, remote signals or barrier semaphores. Data moves between devices by JAX's collectives and lax.ppermute only.
A program may use at most 128 MiB of HBM per device.

v0:
```python
import jax
import jax.numpy as jnp
from jax import lax
from jax.sharding import PartitionSpec as P

HD = 128
SEQS = 4
NODES = 64
CACHE = 1024
ROPE_BASE = 500000.0
MASKED_SCORE = -1e30


def passed_along(block, axis, distance):
    devices = range(lax.axis_size(axis))
    route = [(i - distance, i) for i in devices if i - distance in devices]
    return lax.ppermute(block, axis, route)


def rotate(vectors, positions):
    head_size = vectors.shape[-1]
    half_width = head_size // 2
    exponent = jnp.arange(half_width, dtype=jnp.float32) * (-2.0 / head_size)
    frequency = jnp.exp(exponent * jnp.log(jnp.float32(ROPE_BASE)))
    angles = positions.astype(jnp.float32)[:, None] * frequency[None, :]
    cosine = jnp.cos(angles)[:, None, :]
    sine_of = jnp.sin(angles)[:, None, :]
    front_half = vectors[..., :half_width]
    back_half = vectors[..., half_width:]
    return jnp.concatenate(
        [front_half * cosine - back_half * sine_of, back_half * cosine + front_half * sine_of],
        axis=-1,
    )


def closure(parents):
    node_count = parents.shape[-1]
    node_ids = jnp.arange(node_count, dtype=jnp.int32)
    reached = (parents[:, :, None] == node_ids[None, None, :]).astype(jnp.float32)
    reached = reached + jnp.eye(node_count, dtype=jnp.float32)[None]
    for level_index in range(max(1, (node_count - 1).bit_length())):
        reached = jnp.minimum(
            jnp.einsum("sij,sjk->sik", reached, reached, precision=lax.Precision.HIGHEST), 1.0
        )
    return reached


def partial_attend(queries, all_keys, all_values, visible):
    row_count = queries.shape[0]
    kv_heads = all_keys.shape[1] // HD
    group_size = queries.shape[1] // all_keys.shape[1]
    row_tops = []
    row_totals = []
    mixtures = []
    for kv_head in range(kv_heads):
        query_block = queries[
            :, kv_head * group_size * HD : (kv_head + 1) * group_size * HD
        ].reshape(row_count * group_size, HD)
        key_block = all_keys[:, kv_head * HD : (kv_head + 1) * HD]
        value_block = all_values[:, kv_head * HD : (kv_head + 1) * HD]
        scores = lax.dot_general(
            query_block, key_block, (((1,), (1,)), ((), ())), preferred_element_type=jnp.float32
        )
        scores = scores.reshape(row_count, group_size, -1) * HD ** (-0.5)
        scores = jnp.where(visible[:, None, :], scores, MASKED_SCORE)
        row_top = jnp.max(scores, axis=-1)
        weights = jnp.where(visible[:, None, :], jnp.exp(scores - row_top[..., None]), 0.0)
        row_total = jnp.sum(weights, axis=-1)
        mixed_rows = jnp.dot(
            weights.astype(jnp.bfloat16).reshape(row_count * group_size, -1),
            value_block,
            preferred_element_type=jnp.float32,
        )
        mixed_rows = (
            mixed_rows.reshape(row_count, group_size, HD) / jnp.maximum(row_total, 1.0)[..., None]
        )
        row_tops.append(row_top)
        row_totals.append(row_total)
        mixtures.append(mixed_rows.reshape(row_count, group_size * HD).astype(jnp.bfloat16))
    return (
        jnp.concatenate(row_tops, axis=1),
        jnp.concatenate(row_totals, axis=1),
        jnp.concatenate(mixtures, axis=1),
    )


def finish(tops, totals, parts):
    piece_count, row_count, head_count = tops.shape
    best = jnp.max(tops, axis=0)
    factor = jnp.exp(tops - best[None]) * totals
    denominator = jnp.sum(factor, axis=0)
    numerator = jnp.sum(
        parts.astype(jnp.float32).reshape(piece_count, row_count, head_count, HD)
        * factor[..., None],
        axis=0,
    )
    return (
        (numerator / denominator[..., None])
        .reshape(row_count, head_count * HD)
        .astype(jnp.bfloat16)
    )


def per_device(
    states, q_weight, kv_weight, o_weight, store_keys, store_values, prefix_len, cache_len, parents
):
    inputs = states[0, 0]
    row_count = inputs.shape[0]
    tp_count = lax.axis_size("tp")
    tp_index = lax.axis_index("tp")
    replica = lax.axis_index("rep")
    rep_count = lax.axis_size("rep")
    decoding = lax.axis_index("section") == 1
    own_cols = q_weight.shape[1]
    kv_width = kv_weight.shape[1] // 2
    block_rows = row_count // tp_count
    first_row = tp_index * block_rows
    row_ids = jnp.arange(row_count, dtype=jnp.int32)
    seq_of = row_ids // NODES
    own_prefix = prefix_len[replica]
    reached = closure(parents[0])
    depths = (jnp.sum(reached, axis=-1).astype(jnp.int32) - 1).reshape(row_count)
    seq_lengths = jnp.broadcast_to(cache_len[0][:, None], (SEQS, NODES)).reshape(row_count)
    tree_base = jnp.where(seq_of == 0, own_prefix + row_count, seq_lengths)
    positions = jnp.where(decoding, tree_base + depths, own_prefix + row_ids)
    query_sums = jnp.dot(
        lax.all_gather(inputs, "tp", axis=1, tiled=True),
        q_weight,
        preferred_element_type=jnp.float32,
    )
    own_queries = (
        rotate(query_sums.reshape(row_count, own_cols // HD, HD), positions)
        .reshape(row_count, own_cols)
        .astype(jnp.bfloat16)
    )
    queries = lax.all_gather(own_queries, "tp", axis=1, tiled=True)
    kv_rows = lax.psum_scatter(
        jnp.dot(inputs, kv_weight, preferred_element_type=jnp.float32).astype(jnp.bfloat16),
        "tp",
        scatter_dimension=0,
        tiled=True,
    ).astype(jnp.float32)
    local_pos = lax.dynamic_slice_in_dim(positions, first_row, block_rows, 0)
    new_keys = (
        rotate(kv_rows[:, :kv_width].reshape(block_rows, -1, HD), local_pos)
        .reshape(block_rows, kv_width)
        .astype(jnp.bfloat16)
    )
    new_values = kv_rows[:, kv_width:].astype(jnp.bfloat16)
    moved = passed_along(jnp.stack([new_keys, new_values]), ("section", "rep"), rep_count)
    tail_keys = moved[0]
    tail_values = moved[1]
    store_rows = store_keys.shape[2]
    store_pos = tp_index * store_rows + jnp.arange(store_rows, dtype=jnp.int32)
    prefill_store = jnp.broadcast_to(store_pos[None, :] < own_prefix, (row_count, store_rows))
    decode_store = (store_pos[None, :] // CACHE == seq_of[:, None]) & (
        store_pos[None, :] % CACHE < seq_lengths[:, None]
    )
    block_ids = first_row + jnp.arange(block_rows, dtype=jnp.int32)
    prefill_new = block_ids[None, :] <= row_ids[:, None]
    eye_seq = (jnp.arange(SEQS)[:, None] == jnp.arange(SEQS)[None, :]).astype(jnp.float32)
    tree_full = (eye_seq[:, None, :, None] * reached[:, :, None, :]).reshape(row_count, row_count)
    decode_new = lax.dynamic_slice_in_dim(tree_full, first_row, block_rows, 1) > 0.5
    tail_seen = jnp.broadcast_to((seq_of == 0)[:, None], (row_count, block_rows))
    decode_mask = jnp.concatenate([decode_store, decode_new, tail_seen], axis=1)
    prefill_mask = jnp.concatenate([prefill_store, prefill_new, jnp.zeros_like(tail_seen)], axis=1)
    visible = jnp.where(decoding, decode_mask, prefill_mask)
    all_keys = jnp.concatenate([store_keys[0, 0], new_keys, tail_keys], axis=0)
    all_values = jnp.concatenate([store_values[0, 0], new_values, tail_values], axis=0)
    row_tops, row_totals, mixtures = partial_attend(queries, all_keys, all_values, visible)
    peer_tops, peer_totals, peer_mix = (
        lax.all_to_all(row_tops[None], "tp", split_axis=1, concat_axis=0, tiled=True),
        lax.all_to_all(row_totals[None], "tp", split_axis=1, concat_axis=0, tiled=True),
        lax.all_to_all(
            mixtures[None].astype(jnp.float32), "tp", split_axis=1, concat_axis=0, tiled=True
        ).astype(jnp.bfloat16),
    )
    own_rows = finish(peer_tops, peer_totals, peer_mix)
    result = jnp.dot(
        lax.all_gather(own_rows, "tp", axis=0, tiled=True),
        o_weight,
        preferred_element_type=jnp.float32,
    )
    return result.astype(jnp.bfloat16)[None, None]


def solution(mesh):
    in_specs = (
        P("section", "rep", None, "tp"),
        P(None, "tp"),
        P("tp", None),
        P(None, "tp"),
        P("section", "rep", "tp", None),
        P("section", "rep", "tp", None),
        P(),
        P("rep", None),
        P("rep", None, None),
    )
    out_specs = P("section", "rep", None, "tp")
    return jax.shard_map(
        per_device, mesh=mesh, in_specs=in_specs, out_specs=out_specs, check_vma=False
    )
```

profile of v0, /device:TPU:0, one launch (start us, length us, event | category | flops | bytes accessed | tf_op | source)
XLA Modules:
  0.0 400.3 jit_solution(13573577960373049642)
XLA Ops:
  8.1 2.5 convolution_convert_fusion.1
  10.8 1.1 convolution_minimum_fusion.5
  16.0 69.1 %all-gather.9.cloned.1.call-done = bf16[1,1,256,8192]{3,2,1,0:T(8,128)(2,1)} async-done(((bf16[1,1,256,1024]{3,2,1,0:T(8,128)(2,1)}), bf16[1,1,256,8192]{3,2,1,0:T(8,128)(2,1)}) %all-gather.9.cloned.1.call-update) | async-done | bytes 4194320 | tf_op jit(solution)/shard_map/all_gather | solution.py:127
  85.1 7.0 %fusion = f32[256,512]{1,0:T(8,128)S(1)} fusion(bf16[8192,512]{1,0:T(8,128)(2,1)} %param.10, bf16[1,1,256,8192]{3,2,1,0:T(8,128)(2,1)} %all-gather.9.cloned.1.call-done), kind=kOutput, calls=%fused_computation.9 | convolution fusion | flops 2147483648 | bytes 13107200 | tf_op jit(solution)/shard_map/dot_general | solution.py:126
  95.9 54.1 %reduce-scatter.2.cloned.1.call-done = bf16[32,1024]{1,0:T(8,128)(2,1)} async-done(((bf16[256,1024]{1,0:T(8,128)(2,1)}), bf16[32,1024]{1,0:T(8,128)(2,1)}) %reduce-scatter.2.cloned.1.call-update) | async-done | bytes 65552 | tf_op jit(solution)/shard_map/reduce_scatter | solution.py:137
  151.1 1.3 collective-permute-start
  153.3 1.3 pad_maximum_fusion
  154.6 45.7 %all-gather.5.cloned.1.call-done = bf16[256,4096]{0,1:T(8,128)(2,1)} async-done(((bf16[256,512]{0,1:T(8,128)(2,1)}), bf16[256,4096]{0,1:T(8,128)(2,1)}) %all-gather.5.cloned.1.call-update) | async-done | bytes 2097168 | tf_op jit(solution)/shard_map/all_gather | solution.py:136
  200.3 1.7 fusion.64
  204.8 4.7 %fusion.6 = (f32[256,8]{0,1:T(8,128)S(1)}, f32[256,8]{0,1:T(8,128)S(1)}, f32[256,8]{0,1:T(8,128)S(1)}, f32[256,8]{0,1:T(8,128)S(1)}, f32[256,8,576]{0,2,1:T(8,128)}) fusion(f32[256,8,576]{0,2,1:T(8,128)S(1)} %get-tuple-element.36, f32[256,8]{0,1:T(8,128)S(1)} %get-tuple-element.35, pred[256,576]{0,1:T(8,128)(4,1)S(1)} %add_select_fusion, ...), kind=kOutput, calls=%fused_computation.17 | convolution fusion | flops 318496768 | bytes 19734528 | tf_op jit(solution)/shard_map/dot_general | solution.py:61
  210.1 1.0 reduce.5
  211.9 3.5 all-to-all-start.1
  215.4 7.0 %fusion.8 = (f32[256,8]{0,1:T(8,128)S(1)}, f32[256,8]{0,1:T(8,128)S(1)}, f32[256,8]{0,1:T(8,128)S(1)}) fusion(f32[256,8,576]{0,2,1:T(8,128)} %get-tuple-element.37, f32[256,8]{0,1:T(8,128)S(1)} %get-tuple-element.6, pred[256,576]{0,1:T(8,128)(4,1)S(1)} %add_select_fusion, f32[256,8]{0,1:T(8,128)S(1)} %get-tuple-element.7, f32[256,8,576]{0,2,1:T(8,128)} %copy-done.3, ...), kind=kLoop, calls=%fused_computation.19 | loop fusion | flops 17688576 | bytes 14352384 | tf_op jit(solution)/shard_map/reduce_sum | solution.py:68
  222.4 3.8 divide_convert_fusion.3
  226.2 2.1 divide_convert_fusion.2
  228.3 2.1 divide_convert_fusion.1
  230.4 2.1 divide_convert_fusion
  234.3 1.0 copy.55
  235.3 1.0 copy.56
  236.4 2.5 copy.57
  238.8 3.6 copy.58
  242.5 5.7 %all-to-all-start.2 = ((f32[8,1,1024]{2,1,0:T(1,128)}), f32[8,1,1024]{2,1,0:T(1,128)S(1)}, u32[]{:S(2)}, u32[]{:S(2)}) async-start(f32[8,1,1024]{2,1,0:T(1,128)} %reshape.510), calls=%async_computation.3 | async-start | bytes 65536 | tf_op jit(solution)/shard_map/all_to_all | solution.py:173
  248.2 6.6 %fusion.67 = bf16[256,1,4096]{2,1,0:T(2,128)(2,1)} fusion(bf16[1,256,1024]{2,0,1:T(2,128)(2,1)} %copy.58, bf16[1,256,1024]{2,0,1:T(2,128)(2,1)S(1)} %copy.57, bf16[1,256,1024]{2,0,1:T(2,128)(2,1)S(1)} %copy.56, bf16[1,256,1024]{2,0,1:T(2,128)(2,1)S(1)} %copy.55), kind=kLoop, calls=%fused_computation.139 | loop fusion | flops 8388608 | bytes 4194304
  255.3 13.5 %reduce.2 = bf16[256,4096]{1,0:T(8,128)(2,1)S(1)} reduce(bf16[256,1,4096]{2,1,0:T(2,128)(2,1)} %fusion.67, bf16[]{:T(256)} %broadcast.415), dimensions={1}, to_apply=%fusion.67.reduce_sub_computation | reduce | bytes 4194306
  268.8 3.8 reshape.508
  272.6 6.0 %all-to-all-start = ((bf16[8,2,65536]{2,1,0:T(2,128)(2,1)}), bf16[8,2,65536]{2,1,0:T(2,128)(2,1)S(1)}, u32[]{:S(2)}, u32[]{:S(2)}) async-start(bf16[8,2,65536]{2,1,0:T(2,128)(2,1)} %reshape.508), calls=%async_computation.1 | async-start | bytes 4194304 | tf_op jit(solution)/shard_map/all_to_all | solution.py:174
  280.8 44.4 %all-to-all-done = bf16[8,2,65536]{2,1,0:T(2,128)(2,1)S(1)} async-done(((bf16[8,2,65536]{2,1,0:T(2,128)(2,1)}), bf16[8,2,65536]{2,1,0:T(2,128)(2,1)S(1)}, u32[]{:S(2)}, u32[]{:S(2)}) %all-to-all-start) | async-done | bytes 2097184 | tf_op jit(solution)/shard_map/all_to_all | solution.py:174
  325.2 4.3 %reshape.509 = bf16[256,1,4096]{2,1,0:T(2,128)(2,1)} reshape(bf16[8,2,65536]{2,1,0:T(2,128)(2,1)S(1)} %all-to-all-done) | data formatting | bytes 4194304
  329.5 6.5 %bitcast_convert_fusion = f32[1,256,4096]{2,0,1:T(1,128)S(1)} fusion(bf16[256,1,4096]{2,1,0:T(2,128)(2,1)} %reshape.509), kind=kLoop, calls=%fused_computation.138 | loop fusion | flops 1048576 | bytes 6291456 | tf_op jit(solution)/shard_map/convert_element_type | solution.py:93
  336.0 1.4 multiply_reduce_fusion
  338.5 48.1 %all-gather.7.cloned.1.call-done = bf16[256,4096]{1,0:T(8,128)(2,1)} async-done(((bf16[32,4096]{1,0:T(8,128)(2,1)}), bf16[256,4096]{1,0:T(8,128)(2,1)}) %all-gather.7.cloned.1.call-update) | async-done | bytes 2097168 | tf_op jit(solution)/shard_map/all_gather | solution.py:180
  386.5 7.3 %fusion.26 = bf16[1,1,256,1024]{3,2,1,0:T(8,128)(2,1)} fusion(bf16[256,4096]{1,0:T(8,128)(2,1)} %all-gather.7.cloned.1.call-done, bf16[4096,1024]{1,0:T(8,128)(2,1)} %param.12), kind=kOutput, calls=%fused_computation.35 | convolution fusion | flops 2147745792 | bytes 11010048 | tf_op jit(solution)/shard_map/dot_general | solution.py:179
  (110 shorter events, 20.5 us)
Async XLA Ops:
  6.5 1.6 copy-start
  6.5 6.9 %copy-start.6 = (s32[1,4]{1,0:T(1,128)S(1)}, s32[1,4]{1,0:T(1,128)}, u32[]{:S(2)}) copy-start(s32[1,4]{1,0:T(1,128)} %param.16) | copy-start | bytes 52
  6.5 7.0 %copy-start.7 = (s32[2]{0:T(128)S(1)}, s32[2]{0:T(128)}, u32[]{:S(2)}) copy-start(s32[2]{0:T(128)} %param.15) | copy-start | bytes 28
  6.5 78.5 %all-gather.9.cloned.1.call-start = ((), (), s32[]{:S(2)}) async-start(), calls=%async_computation.7 | async-start | bytes 4718592 | tf_op jit(solution)/shard_map/all_gather | solution.py:127
  7.3 142.8 %reduce-scatter.2.cloned.1.call-start = ((), (), s32[]{:S(2)}) async-start(), calls=%async_computation.5 | async-start | bytes 589824 | tf_op jit(solution)/shard_map/reduce_scatter | solution.py:137
  10.7 189.6 %all-gather.5.cloned.1.call-start = ((), (), s32[]{:S(2)}) async-start(), calls=%async_computation.4 | async-start | bytes 2359296 | tf_op jit(solution)/shard_map/all_gather | solution.py:136
  151.1 2.2 collective-permute-start
  202.7 2.2 copy-start.3
  203.4 6.0 %copy-start.2 = (f32[256,8,576]{0,2,1:T(8,128)}, f32[256,8,576]{0,2,1:T(8,128)S(1)}, u32[]{:S(2)}) copy-start(f32[256,8,576]{0,2,1:T(8,128)S(1)} %fusion.36) | copy-start | bytes 14155780
  204.3 5.2 %copy-start.4 = (f32[256,8,576]{0,2,1:T(8,128)}, f32[256,8,576]{0,2,1:T(8,128)S(1)}, u32[]{:S(2)}) copy-start(f32[256,8,576]{0,2,1:T(8,128)S(1)} %get-tuple-element.36) | copy-start | bytes 14155780
  210.1 16.1 %slice-start.4 = ((s8[4718592]{0:T(1024)(128)(4,1)}), s8[524288]{0:T(1024)(128)(4,1)S(1)}, s32[]{:S(2)}) async-start(s8[4718592]{0:T(1024)(128)(4,1)} %bitcast.102), calls=%async_computation.12 | async-start | bytes 1048576
  211.9 30.6 %all-to-all-start.1 = ((f32[8,1,1024]{2,1,0:T(1,128)}), f32[8,1,1024]{2,1,0:T(1,128)S(1)}, u32[]{:S(2)}, u32[]{:S(2)}) async-start(f32[8,1,1024]{2,1,0:T(1,128)} %reshape.512), calls=%async_computation.2 | async-start | bytes 65536 | tf_op jit(solution)/shard_map/all_to_all | solution.py:172
  215.4 10.8 %slice-start.5 = ((s8[4718592]{0:T(1024)(128)(4,1)}), s8[4194304]{0:T(1024)(128)(4,1)S(1)}, s32[]{:S(2)}) async-start(s8[4718592]{0:T(1024)(128)(4,1)} %bitcast.102), calls=%async_computation.13 | async-start | bytes 8388608
  222.4 5.9 %slice-start.2 = ((s8[4718592]{0:T(1024)(128)(4,1)}), s8[4194304]{0:T(1024)(128)(4,1)S(1)}, s32[]{:S(2)}) async-start(s8[4718592]{0:T(1024)(128)(4,1)} %bitcast.99), calls=%async_computation.10 | async-start | bytes 8388608
  226.2 2.1 slice-start.3
  226.2 4.2 %slice-start = ((s8[4718592]{0:T(1024)(128)(4,1)}), s8[4194304]{0:T(1024)(128)(4,1)S(1)}, s32[]{:S(2)}) async-start(s8[4718592]{0:T(1024)(128)(4,1)} %bitcast.97), calls=%async_computation.8 | async-start | bytes 8388608
  228.3 2.1 slice-start.1
  230.4 4.9 %copy-start.5 = (bf16[256,8,128]{0,2,1:T(8,128)(2,1)S(1)}, bf16[256,8,128]{0,2,1:T(8,128)(2,1)}, u32[]{:S(2)}) copy-start(bf16[256,8,128]{0,2,1:T(8,128)(2,1)} %divide_convert_fusion.2) | copy-start | bytes 1572868
  242.5 30.1 %all-to-all-start.2 = ((f32[8,1,1024]{2,1,0:T(1,128)}), f32[8,1,1024]{2,1,0:T(1,128)S(1)}, u32[]{:S(2)}, u32[]{:S(2)}) async-start(f32[8,1,1024]{2,1,0:T(1,128)} %reshape.510), calls=%async_computation.3 | async-start | bytes 65536 | tf_op jit(solution)/shard_map/all_to_all | solution.py:173
  272.6 52.6 %all-to-all-start = ((bf16[8,2,65536]{2,1,0:T(2,128)(2,1)}), bf16[8,2,65536]{2,1,0:T(2,128)(2,1)S(1)}, u32[]{:S(2)}, u32[]{:S(2)}) async-start(bf16[8,2,65536]{2,1,0:T(2,128)(2,1)} %reshape.508), calls=%async_computation.1 | async-start | bytes 4194304 | tf_op jit(solution)/shard_map/all_to_all | solution.py:174
  278.6 108.0 %all-gather.7.cloned.1.call-start = ((), (), s32[]{:S(2)}) async-start(), calls=%async_computation.6 | async-start | bytes 2359296 | tf_op jit(solution)/shard_map/all_gather | solution.py:180
  386.5 7.3 %copy-start.1 = (bf16[1024,1024]{1,0:T(8,128)(2,1)S(1)}, bf16[1024,1024]{1,0:T(8,128)(2,1)}, u32[]{:S(2)}) copy-start(bf16[1024,1024]{1,0:T(8,128)(2,1)} %param.11) | copy-start | bytes 6291460
Sparse Core Ops, SparseCore 0:
  9.5 75.4 all-gather.8
  88.4 61.5 reduce-scatter.1
  152.2 48.0 all-gather.4
  338.6 47.8 all-gather.6
where the time goes:
time: 401 us; the launch traced here: 400 us
  waiting for transfers between devices  263 us (66%)
  other arithmetic  44.4 us (11%)
  matrix products  36.4 us (9%)
  local copies, waits for them, and re-layouts  25.7 us (6%)
  starting transfers between devices  16.9 us (4%)
  between operations  14.3 us (4%)
    all_gather x1, waiting for transfers between devices, per_device(): lax.all_gather(inputs, 'tp', axis=1, tiled=True)  69.1 us
    reduce_scatter x1, waiting for transfers between devices, per_device(): lax.psum_scatter(jnp.dot(inputs, kv_weight, preferred_element_type=jnp.fl...  54.1 us
    all_gather x1, waiting for transfers between devices, per_device(): lax.all_gather(own_rows, 'tp', axis=0, tiled=True)  48.1 us
    all_gather x1, waiting for transfers between devices, per_device(): queries = lax.all_gather(own_queries, 'tp', axis=1, tiled=True)  45.7 us
    all_to_all x1, waiting for transfers between devices, per_device(): lax.all_to_all(mixtures[None].astype(jnp.float32), 'tp', split_axis=1, co...  44.4 us
    unnamed x7, other arithmetic  22 us
    unnamed x38, local copies, waits for them, and re-layouts  13.2 us
    dot_general x4, matrix products, partial_attend(): jnp.dot(weights.astype(jnp.bfloat16).reshape(row_count * group_size, -1),...  10.1 us
  transfers between devices with their start and end apart: 8, of which 6 were waited for; matrix products, arithmetic and copies ran while one was open for 18% of the time, Pallas kernels for 0%

commit v1 on v0

--- a/solution.py
+++ b/solution.py
@@ -9,6 +9,13 @@
 CACHE = 1024
 ROPE_BASE = 500000.0
 MASKED_SCORE = -1e30
+
+
+def trade_parts(array, axis, split, join):
+    n_dev = lax.axis_size(axis)
+    blocks = jnp.stack(jnp.split(array, n_dev, axis=split), axis=0)
+    blocks = lax.all_to_all(blocks, axis, split_axis=0, concat_axis=0)
+    return jnp.concatenate(blocks, axis=join)
 
 
 def passed_along(block, axis, distance):
@@ -171,9 +178,7 @@
     peer_tops, peer_totals, peer_mix = (
         lax.all_to_all(row_tops[None], "tp", split_axis=1, concat_axis=0, tiled=True),
         lax.all_to_all(row_totals[None], "tp", split_axis=1, concat_axis=0, tiled=True),
-        lax.all_to_all(
-            mixtures[None].astype(jnp.float32), "tp", split_axis=1, concat_axis=0, tiled=True
-        ).astype(jnp.bfloat16),
+        trade_parts(mixtures[None].astype(jnp.float32), "tp", 1, 0).astype(jnp.bfloat16),
     )
     own_rows = finish(peer_tops, peer_totals, peer_mix)
     result = jnp.dot(

time: 401 us -> 374 us (0.933)
  other arithmetic: 44.4 us -> 20.4 us
  starting transfers between devices: 16.9 us -> 11.7 us
    unnamed x7 -> x3, other arithmetic: 22 us -> 1.92 us
    all_to_all x1, waiting for transfers between devices: 44.4 us -> 35.1 us  [trade_parts(): blocks = lax.all_to_all(blocks, axis, split_axis=0, concat_axis=0)]
    mul x0 -> x3, local copies, waits for them, and re-layouts: none -> 7.86 us  [the longest x2 7.76 us: finish(): parts.astype(jnp.float32).reshape(piece_count, row_count, head_count, HD)]
    all_to_all x1, waiting for transfers between devices: 0.01 us -> 5.89 us  [per_device(): lax.all_to_all(row_totals[None], 'tp', split_axis=1, concat_axis=0, tiled...]
    concatenate x4, local copies, waits for them, and re-layouts: 8.09 us -> 2.44 us  [partial_attend(): jnp.concatenate(mixtures, axis=1)]
    convert_element_type x1, other arithmetic: 6.5 us -> 1.37 us  [per_device(): mixtures[None].astype(jnp.float32)]
    all_to_all x1, waiting for transfers between devices: 0.01 us -> 4.81 us  [per_device(): lax.all_to_all(row_tops[None], 'tp', split_axis=1, concat_axis=0, tiled=T...]
    unnamed x38 -> x34, local copies, waits for them, and re-layouts: 13.2 us -> 9.48 us
  transfers between devices with their start and end apart: 8 -> 8, of which waited for: 6 -> 8; matrix products, arithmetic and copies ran while one was open for 18% -> 9% of each run, Pallas kernels for 0% -> 0%
where the time goes in v1:
time: 374 us; the launch traced here: 373 us
  waiting for transfers between devices  264 us (71%)
  matrix products  36.1 us (10%)
  local copies, waits for them, and re-layouts  26.2 us (7%)
  other arithmetic  20.4 us (5%)
  between operations  14.3 us (4%)
  starting transfers between devices  11.7 us (3%)
    all_gather x1, waiting for transfers between devices, per_device(): lax.all_gather(inputs, 'tp', axis=1, tiled=True)  69.2 us
    reduce_scatter x1, waiting for transfers between devices, per_device(): lax.psum_scatter(jnp.dot(inputs, kv_weight, preferred_element_type=jnp.fl...  54.2 us
    all_gather x1, waiting for transfers between devices, per_device(): lax.all_gather(own_rows, 'tp', axis=0, tiled=True)  48.1 us
    all_gather x1, waiting for transfers between devices, per_device(): queries = lax.all_gather(own_queries, 'tp', axis=1, tiled=True)  45.7 us
    all_to_all x1, waiting for transfers between devices, trade_parts(): blocks = lax.all_to_all(blocks, axis, split_axis=0, concat_axis=0)  35.1 us
    dot_general x4, matrix products, partial_attend(): jnp.dot(weights.astype(jnp.bfloat16).reshape(row_count * group_size, -1),...  9.8 us
    unnamed x34, local copies, waits for them, and re-layouts  9.48 us
    mul x2, local copies, waits for them, and re-layouts, finish(): parts.astype(jnp.float32).reshape(piece_count, row_count, head_count, HD)  7.76 us
  transfers between devices with their start and end apart: 8, of which 8 were waited for; matrix products, arithmetic and copies ran while one was open for 9% of the time, Pallas kernels for 0%

profile of v1, /device:TPU:0, one launch (start us, length us, event | category | flops | bytes accessed | tf_op | source)
XLA Modules:
  0.0 373.1 jit_solution(816997513177283953)
XLA Ops:
  8.1 2.5 convolution_convert_fusion.1
  10.8 1.1 convolution_minimum_fusion.5
  15.8 69.2 %all-gather.9.cloned.1.call-done = bf16[1,1,256,8192]{3,2,1,0:T(8,128)(2,1)} async-done(((bf16[1,1,256,1024]{3,2,1,0:T(8,128)(2,1)}), bf16[1,1,256,8192]{3,2,1,0:T(8,128)(2,1)}) %all-gather.9.cloned.1.call-update) | async-done | bytes 4194320 | tf_op jit(solution)/shard_map/all_gather | solution.py:134
  85.1 7.0 %fusion = f32[256,512]{1,0:T(8,128)S(1)} fusion(bf16[8192,512]{1,0:T(8,128)(2,1)} %param.10, bf16[1,1,256,8192]{3,2,1,0:T(8,128)(2,1)} %all-gather.9.cloned.1.call-done), kind=kOutput, calls=%fused_computation.8 | convolution fusion | flops 2147483648 | bytes 13107200 | tf_op jit(solution)/shard_map/dot_general | solution.py:133
  95.8 54.2 %reduce-scatter.2.cloned.1.call-done = bf16[32,1024]{1,0:T(8,128)(2,1)} async-done(((bf16[256,1024]{1,0:T(8,128)(2,1)}), bf16[32,1024]{1,0:T(8,128)(2,1)}) %reduce-scatter.2.cloned.1.call-update) | async-done | bytes 65552 | tf_op jit(solution)/shard_map/reduce_scatter | solution.py:144
  151.1 1.3 collective-permute-start
  153.3 1.3 pad_maximum_fusion
  154.6 45.7 %all-gather.5.cloned.1.call-done = bf16[256,4096]{0,1:T(8,128)(2,1)} async-done(((bf16[256,512]{0,1:T(8,128)(2,1)}), bf16[256,4096]{0,1:T(8,128)(2,1)}) %all-gather.5.cloned.1.call-update) | async-done | bytes 2097168 | tf_op jit(solution)/shard_map/all_gather | solution.py:143
  200.3 1.7 fusion.73
  204.8 4.7 %fusion.6 = (f32[256,8]{0,1:T(8,128)S(1)}, f32[256,8]{0,1:T(8,128)S(1)}, f32[256,8]{0,1:T(8,128)S(1)}, f32[256,8]{0,1:T(8,128)S(1)}, f32[256,8,576]{0,2,1:T(8,128)}) fusion(f32[256,8,576]{0,2,1:T(8,128)S(1)} %get-tuple-element.36, f32[256,8]{0,1:T(8,128)S(1)} %get-tuple-element.35, pred[256,576]{0,1:T(8,128)(4,1)S(1)} %add_select_fusion, ...), kind=kOutput, calls=%fused_computation.15 | convolution fusion | flops 318496768 | bytes 19734528 | tf_op jit(solution)/shard_map/dot_general | solution.py:68
  209.5 1.3 divide_convert_fusion.3
  211.1 7.0 %fusion.8 = (f32[256,8]{0,1:T(8,128)S(1)}, f32[256,8]{0,1:T(8,128)S(1)}, f32[256,8]{0,1:T(8,128)S(1)}) fusion(f32[256,8,576]{0,2,1:T(8,128)} %get-tuple-element.37, f32[256,8]{0,1:T(8,128)S(1)} %get-tuple-element.6, pred[256,576]{0,1:T(8,128)(4,1)S(1)} %add_select_fusion, f32[256,8]{0,1:T(8,128)S(1)} %get-tuple-element.7, f32[256,8,576]{0,2,1:T(8,128)} %copy-done.3, ...), kind=kLoop, calls=%fused_computation.17 | loop fusion | flops 17688576 | bytes 14352384 | tf_op jit(solution)/shard_map/reduce_sum | solution.py:75
  218.1 1.3 divide_convert_fusion.2
  219.6 3.6 divide_convert_fusion.1
  223.2 1.0 copy.55
  224.2 3.6 divide_convert_fusion
  227.9 1.0 copy.56
  228.9 1.4 maximum_convert_fusion
  236.0 1.0 reduce.3
  237.7 3.3 all-to-all-start.1
  241.2 1.0 reduce.1
  242.9 4.8 %all-to-all-done.1 = f32[8,1,1024]{2,1,0:T(1,128)S(1)} async-done(((f32[8,1,1024]{2,1,0:T(1,128)}), f32[8,1,1024]{2,1,0:T(1,128)S(1)}, u32[]{:S(2)}, u32[]{:S(2)}) %all-to-all-start.1) | async-done | bytes 32800 | tf_op jit(solution)/shard_map/all_to_all | solution.py:179
  247.7 3.3 all-to-all-start.2
  251.7 5.9 %all-to-all-done.2 = f32[8,1,1024]{2,1,0:T(1,128)S(1)} async-done(((f32[8,1,1024]{2,1,0:T(1,128)}), f32[8,1,1024]{2,1,0:T(1,128)S(1)}, u32[]{:S(2)}, u32[]{:S(2)}) %all-to-all-start.2) | async-done | bytes 32800 | tf_op jit(solution)/shard_map/all_to_all | solution.py:180
  257.6 3.6 all-to-all-start
  263.7 2.8 mul.197
  266.5 4.9 %mul.198 = f32[8,1,32,4096]{3,2,1,0:T(8,128)} reshape(f32[8,32,32,128]{3,2,1,0:T(8,128)} %mul.197) | data formatting | bytes 8388608 | tf_op jit(solution)/shard_map/mul | solution.py:100
  271.4 35.1 %all-to-all-done = bf16[8,1,32,4096]{3,2,1,0:T(8,128)(2,1)S(1)} async-done(((bf16[8,1,32,4096]{3,2,1,0:T(8,128)(2,1)}), bf16[8,1,32,4096]{3,2,1,0:T(8,128)(2,1)S(1)}, u32[]{:S(2)}, u32[]{:S(2)}) %all-to-all-start) | async-done | bytes 2097184 | tf_op jit(solution)/shard_map/all_to_all | solution.py:17
  306.6 2.8 multiply_reduce_fusion
  310.1 1.0 copy.64
  311.2 48.1 %all-gather.7.cloned.1.call-done = bf16[256,4096]{1,0:T(8,128)(2,1)} async-done(((bf16[32,4096]{1,0:T(8,128)(2,1)}), bf16[256,4096]{1,0:T(8,128)(2,1)}) %all-gather.7.cloned.1.call-update) | async-done | bytes 2097168 | tf_op jit(solution)/shard_map/all_gather | solution.py:185
  359.3 7.3 %fusion.27 = bf16[1,1,256,1024]{3,2,1,0:T(8,128)(2,1)} fusion(bf16[256,4096]{1,0:T(8,128)(2,1)} %all-gather.7.cloned.1.call-done, bf16[4096,1024]{1,0:T(8,128)(2,1)} %param.12), kind=kOutput, calls=%fused_computation.36 | convolution fusion | flops 2147745792 | bytes 11010048 | tf_op jit(solution)/shard_map/dot_general | solution.py:184
  (110 shorter events, 25.1 us)
Async XLA Ops:
  6.5 1.6 copy-start
  6.5 6.9 %copy-start.6 = (s32[1,4]{1,0:T(1,128)S(1)}, s32[1,4]{1,0:T(1,128)}, u32[]{:S(2)}) copy-start(s32[1,4]{1,0:T(1,128)} %param.16) | copy-start | bytes 52
  6.5 7.0 %copy-start.7 = (s32[2]{0:T(128)S(1)}, s32[2]{0:T(128)}, u32[]{:S(2)}) copy-start(s32[2]{0:T(128)} %param.15) | copy-start | bytes 28
  6.5 78.5 %all-gather.9.cloned.1.call-start = ((), (), s32[]{:S(2)}) async-start(), calls=%async_computation.7 | async-start | bytes 4718592 | tf_op jit(solution)/shard_map/all_gather | solution.py:134
  7.3 142.8 %reduce-scatter.2.cloned.1.call-start = ((), (), s32[]{:S(2)}) async-start(), calls=%async_computation.5 | async-start | bytes 589824 | tf_op jit(solution)/shard_map/reduce_scatter | solution.py:144
  10.7 189.6 %all-gather.5.cloned.1.call-start = ((), (), s32[]{:S(2)}) async-start(), calls=%async_computation.4 | async-start | bytes 2359296 | tf_op jit(solution)/shard_map/all_gather | solution.py:143
  151.1 2.2 collective-permute-start
  154.6 54.9 %copy-start.4 = (bf16[576,512]{1,0:T(8,128)(2,1)}, bf16[576,512]{1,0:T(8,128)(2,1)S(1)}, u32[]{:S(2)}) copy-start(bf16[576,512]{1,0:T(8,128)(2,1)S(1)} %get-tuple-element.43) | copy-start | bytes 1769476
  202.7 2.1 copy-start.2
  203.5 6.0 %copy-start.3 = (f32[256,8,576]{0,2,1:T(8,128)}, f32[256,8,576]{0,2,1:T(8,128)S(1)}, u32[]{:S(2)}) copy-start(f32[256,8,576]{0,2,1:T(8,128)S(1)} %fusion.46) | copy-start | bytes 14155780
  210.8 7.2 %slice-start = ((s8[4718592]{0:T(1024)(128)(4,1)}), s8[524288]{0:T(1024)(128)(4,1)S(1)}, s32[]{:S(2)}) async-start(s8[4718592]{0:T(1024)(128)(4,1)} %bitcast.126), calls=%async_computation.8 | async-start | bytes 1048576
  211.0 7.0 %slice-start.1 = ((s8[4718592]{0:T(1024)(128)(4,1)}), s8[4194304]{0:T(1024)(128)(4,1)S(1)}, s32[]{:S(2)}) async-start(s8[4718592]{0:T(1024)(128)(4,1)} %bitcast.126), calls=%async_computation.9 | async-start | bytes 8388608
  211.1 7.0 %copy-start.5 = (bf16[576,512]{1,0:T(8,128)(2,1)S(1)}, bf16[576,512]{1,0:T(8,128)(2,1)}, u32[]{:S(2)}) copy-start(bf16[576,512]{1,0:T(8,128)(2,1)} %copy-done.4) | copy-start | bytes 1769476
  237.7 10.0 %all-to-all-start.1 = ((f32[8,1,1024]{2,1,0:T(1,128)}), f32[8,1,1024]{2,1,0:T(1,128)S(1)}, u32[]{:S(2)}, u32[]{:S(2)}) async-start(f32[8,1,1024]{2,1,0:T(1,128)} %reshape.492), calls=%async_computation.2 | async-start | bytes 65536 | tf_op jit(solution)/shard_map/all_to_all | solution.py:179
  247.7 10.0 %all-to-all-start.2 = ((f32[8,1,1024]{2,1,0:T(1,128)}), f32[8,1,1024]{2,1,0:T(1,128)S(1)}, u32[]{:S(2)}, u32[]{:S(2)}) async-start(f32[8,1,1024]{2,1,0:T(1,128)} %reshape.490), calls=%async_computation.3 | async-start | bytes 65536 | tf_op jit(solution)/shard_map/all_to_all | solution.py:180
  257.6 48.9 %all-to-all-start = ((bf16[8,1,32,4096]{3,2,1,0:T(8,128)(2,1)}), bf16[8,1,32,4096]{3,2,1,0:T(8,128)(2,1)S(1)}, u32[]{:S(2)}, u32[]{:S(2)}) async-start(bf16[8,1,32,4096]{3,2,1,0:T(8,128)(2,1)} %fusion.36), calls=%async_computation.1 | async-start | bytes 4194304 | tf_op jit(solution)/shard_map/all_to_all | solution.py:17
  261.2 98.0 %all-gather.7.cloned.1.call-start = ((), (), s32[]{:S(2)}) async-start(), calls=%async_computation.6 | async-start | bytes 2359296 | tf_op jit(solution)/shard_map/all_gather | solution.py:185
  359.3 7.3 %copy-start.1 = (bf16[1024,1024]{1,0:T(8,128)(2,1)S(1)}, bf16[1024,1024]{1,0:T(8,128)(2,1)}, u32[]{:S(2)}) copy-start(bf16[1024,1024]{1,0:T(8,128)(2,1)} %param.11) | copy-start | bytes 6291460
Sparse Core Ops, SparseCore 0:
  9.5 75.4 all-gather.8
  88.4 61.6 reduce-scatter.1
  152.2 48.0 all-gather.4
  311.3 47.9 all-gather.6
